TPU v7x, 32 devices: a whole 2x2x4 slice. The times are simulated.
32 devices in a mesh: groups: 2 (over y), ctx: 4 (over z), heads: 2 (over x), rep: 2 (over core).
Axes of the slice: x: 2, y: 2, z: 4, core: 2. Of those that a mesh axis runs over, the one named last changes fastest.
Arguments:
- queries: bfloat16 [256, 128, 128], P(('groups', 'ctx', 'rep'), 'heads'), parts along dimension 0, may hold values from -10 to 10
- cache_keys: bfloat16 [16384, 8, 128], P(('groups', 'ctx'), 'heads'), parts along dimension 0, may hold values from -10 to 10
- cache_values: bfloat16 [16384, 8, 128], P(('groups', 'ctx'), 'heads'), parts along dimension 0, may hold values from -6 to 6
- new_keys: bfloat16 [256, 8, 128], P(('groups', 'ctx', 'rep'), 'heads'), parts along dimension 0, may hold values from -6 to 6
- new_values: bfloat16 [256, 8, 128], P(('groups', 'ctx', 'rep'), 'heads'), parts along dimension 0, may hold values from -6 to 6
- positions: int32 [256], P(('groups', 'ctx', 'rep')), parts along dimension 0, may hold values from 2 to 8191
- cached_length: int32 [2], P('groups'), parts along dimension 0, may hold values from 4096 to 8192
- out_weight: bfloat16 [16384, 16384], P('heads', ('ctx', 'rep')), may hold values from -0.046875 to 0.046875
Outputs:
- mixed: bfloat16 [256, 16384], P(('groups', 'heads'), ('ctx', 'rep')), parts along dimension 0
There are 2 independent parts, one for each index of `groups`. A program takes and returns all parts, laid end to end along the dimension named above; an argument that names none is the same for every part. Nothing has to cross between parts.
All inputs are finite; a program needn't handle non-finite values.
Results may differ from a plain program's by a relative error of at most 0.0052.
Values may be sent and summed in bfloat16 or wider, within the bound.
A program may use at most 128 MiB of HBM per device.

v0:
```python
import jax
import jax.numpy as jnp
from jax import lax
from jax.sharding import PartitionSpec as P

NEG_FILL = -1e30


def shifted(value, axis, steps):
    count = lax.axis_size(axis)
    pairs = [(source, (source + steps) % count) for source in range(count)]
    return lax.ppermute(value, axis, pairs)


def combine(state, update):
    maxima, totals, values = state
    new_max, new_tot, new_val = update
    highest = jnp.maximum(maxima, new_max)
    keeping = jnp.exp(maxima - highest)
    taking = jnp.exp(new_max - highest)
    return (
        highest,
        keeping * totals + taking * new_tot,
        keeping[..., None] * values + taking[..., None] * new_val,
    )


def local(
    queries, cache_keys, cache_values, new_keys, new_values, positions, cached_length, out_weight
):
    token_rows, local_heads, head_size = queries.shape
    block_len, local_kv = (cache_keys.shape[0], cache_keys.shape[1])
    per_group = local_heads // local_kv
    scale_factor = head_size ** (-0.5)
    cycle_size = lax.axis_size("ctx")
    kv_start = lax.axis_index("ctx") * block_len
    limits = jnp.minimum(cached_length[0], positions)
    slot_index = kv_start + jnp.arange(block_len, dtype=jnp.int32)

    def attend(visitor, bounds):
        rows = visitor.shape[0]
        grouped = visitor.reshape(rows, local_kv, per_group, head_size)
        scores = (
            jnp.einsum("tkgd,jkd->tkgj", grouped, cache_keys, preferred_element_type=jnp.float32)
            * scale_factor
        )
        visible = (slot_index[None, :] < bounds[:, None])[:, None, None, :]
        scores = jnp.where(visible, scores, NEG_FILL)
        maxima = jnp.max(scores, axis=-1)
        weights = jnp.where(visible, jnp.exp(scores - maxima[..., None]), 0.0)
        totals = jnp.sum(weights, axis=-1)
        output = jnp.einsum(
            "tkgj,jkd->tkgd",
            weights.astype(jnp.bfloat16),
            cache_values,
            preferred_element_type=jnp.float32,
        )
        return (
            maxima.reshape(rows, local_heads),
            totals.reshape(rows, local_heads),
            output.reshape(rows, local_heads, head_size),
        )

    def partial_value(visitor, bounds):
        return attend(visitor, bounds)

    grouped_home = queries.reshape(token_rows, local_kv, per_group, head_size)
    own_score = (
        jnp.einsum("tkgd,tkd->tkg", grouped_home, new_keys, preferred_element_type=jnp.float32)
        * scale_factor
    )
    own_score = own_score.reshape(token_rows, local_heads)
    own_values = jnp.broadcast_to(
        new_values.astype(jnp.float32)[:, :, None, :], (token_rows, local_kv, per_group, head_size)
    ).reshape(token_rows, local_heads, head_size)
    start_state = (own_score, jnp.ones((token_rows, local_heads), jnp.float32), own_values)

    def travel(step, carry):
        visitor, bounds, state = carry
        state = combine(state, partial_value(visitor, bounds))
        visitor, bounds = shifted((visitor, bounds), "ctx", 1)
        state = shifted((state[0], state[1], state[2]), "ctx", 1)
        return (visitor, bounds, state)

    _, _, final = lax.fori_loop(0, cycle_size, travel, (queries, limits, start_state))
    attended = (
        (final[2] / final[1][..., None])
        .astype(jnp.bfloat16)
        .reshape(token_rows, local_heads * head_size)
    )
    terms = jnp.dot(
        lax.all_gather(attended, ("ctx", "rep"), axis=0, tiled=True),
        out_weight,
        preferred_element_type=jnp.float32,
    )
    return lax.psum_scatter(terms, "heads", scatter_dimension=0, tiled=True).astype(jnp.bfloat16)


def solution(mesh):
    return jax.shard_map(
        local,
        mesh=mesh,
        in_specs=(
            P(("groups", "ctx", "rep"), "heads", None),
            P(("groups", "ctx"), "heads", None),
            P(("groups", "ctx"), "heads", None),
            P(("groups", "ctx", "rep"), "heads", None),
            P(("groups", "ctx", "rep"), "heads", None),
            P(("groups", "ctx", "rep")),
            P("groups"),
            P("heads", ("ctx", "rep")),
        ),
        out_specs=P(("groups", "heads"), ("ctx", "rep")),
        check_vma=False,
    )
```

profile of v0, /device:TPU:0, one launch (start us, length us, event | category | flops | bytes accessed | tf_op | source)
XLA Modules:
  0.0 231.2 jit_solution(15120731785396124283)
XLA Ops:
  6.5 1.7 copy.71
  8.3 1.2 fusion.21
  9.5 1.9 copy.27
  11.4 3.2 %copy.28 = bf16[2048,4,128]{2,0,1:T(8,128)(2,1)} copy(bf16[2048,4,128]{2,1,0:T(4,128)(2,1)} %param.12) | data formatting | bytes 4194304
  15.4 142.7 %while.19 = (s32[]{:T(128)}, bf16[16,64,128]{2,1,0:T(8,128)(2,1)}, s32[16]{0:T(128)S(1)}, f32[16,64]{1,0:T(8,128)S(1)}, f32[16,64]{1,0:T(8,128)S(1)}, /*index=5*...) while((s32[]{:T(128)}, bf16[16,64,128]{2,1,0:T(8,128)(2,1)}, ...), condition=%wide.region_3.4_spmd.clone, body=%wide.region_0.3_spmd.clone.sunk | while | flops 1101436928 | bytes 70263568 | solution.py:85
  15.4 1.0 copy.57
  16.5 1.6 fusion.35
  18.1 3.2 %copy-done.1 = f32[4,2048,16,16]{1,3,2,0:T(8,128)} copy-done((f32[4,2048,16,16]{1,3,2,0:T(8,128)}, f32[4,2048,16,16]{1,3,2,0:T(8,128)S(1)}, u32[]{:S(2)}) %copy-start.1) | copy-done | bytes 8388632 | tf_op jit(solution)/shard_map/while
  21.3 2.7 %fusion.36 = f32[16,4,16]{2,0,1:T(8,128)S(1)} fusion(f32[4,2048,16,16]{1,3,2,0:T(8,128)S(1)} %get-tuple-element.197, f32[16,4,16]{2,0,1:T(8,128)S(1)} %get-tuple-element.198, pred[16,2048]{1,0:T(8,128)(4,1)S(1)} %broadcast_compare_fusion.2), kind=kLoop, calls=%fused_computation.5.clone.1 | loop fusion | flops 10484736 | bytes 8429568 | tf_op jit(solution)/shard_map/while/body/eval_jaxpr/reduce_sum | solution.py:51
  24.2 5.5 %fusion.37 = f32[16,4,16,128]{3,2,0,1:T(8,128)S(1)} fusion(bf16[2048,4,128]{2,0,1:T(8,128)(2,1)} %get-tuple-element.230, f32[4,2048,16,16]{1,3,2,0:T(8,128)} %copy-done.1, f32[16,4,16]{2,0,1:T(8,128)S(1)} %get-tuple-element.198, pred[16,2048]{1,0:T(8,128)(4,1)S(1)} %broadcast_compare_fusion.2), kind=kOutput, calls=%fused_computation.11.clone.1 | convolution fusion | flops 547356672 | bytes 11046912 | tf_op jit(solution)/shard_map/while/body/eval_jaxpr/tkgj,jkd->tkgd/dot_general | solution.py:52
  29.8 0.3 fusion.38
  30.1 3.1 %collective-permute-start.4 = (f32[16,64,128]{2,1,0:T(8,128)S(1)}, f32[16,64,128]{2,1,0:T(8,128)S(1)}, u32[]{:S(2)}, u32[]{:S(2)}) collective-permute-start(f32[16,64,128]{2,1,0:T(8,128)S(1)} %fusion.38), channel_id=1, source_target_pairs={{0,4},{4,8},{8,12},{12,0},{1,5},{5,9},{9,13},{13,1},{2,6},{6,10},{... | collective-permute-start | bytes 1572872 | tf_op jit(solution)/shard_map/while/body/eval_jaxpr/ppermute | solution.py:12
  33.2 1.6 collective-permute-start
  34.8 1.6 collective-permute-start.2
  36.4 1.7 collective-permute-start.1
  38.2 15.1 %collective-permute-done.1 = s32[16]{0:T(128)S(1)} collective-permute-done((s32[16]{0:T(128)S(1)}, s32[16]{0:T(128)S(1)}, u32[]{:S(2)}, u32[]{:S(2)}) %collective-permute-start.1) | collective-permute-done | bytes 96 | tf_op jit(solution)/shard_map/while/body/eval_jaxpr/ppermute | solution.py:12
  53.3 1.0 copy.57
  54.3 1.6 fusion.35
  56.0 3.2 %copy-done.1 = f32[4,2048,16,16]{1,3,2,0:T(8,128)} copy-done((f32[4,2048,16,16]{1,3,2,0:T(8,128)}, f32[4,2048,16,16]{1,3,2,0:T(8,128)S(1)}, u32[]{:S(2)}) %copy-start.1) | copy-done | bytes 8388632 | tf_op jit(solution)/shard_map/while
  59.2 2.7 %fusion.36 = f32[16,4,16]{2,0,1:T(8,128)S(1)} fusion(f32[4,2048,16,16]{1,3,2,0:T(8,128)S(1)} %get-tuple-element.197, f32[16,4,16]{2,0,1:T(8,128)S(1)} %get-tuple-element.198, pred[16,2048]{1,0:T(8,128)(4,1)S(1)} %broadcast_compare_fusion.2), kind=kLoop, calls=%fused_computation.5.clone.1 | loop fusion | flops 10484736 | bytes 8429568 | tf_op jit(solution)/shard_map/while/body/eval_jaxpr/reduce_sum | solution.py:51
  62.1 5.5 %fusion.37 = f32[16,4,16,128]{3,2,0,1:T(8,128)S(1)} fusion(bf16[2048,4,128]{2,0,1:T(8,128)(2,1)} %get-tuple-element.230, f32[4,2048,16,16]{1,3,2,0:T(8,128)} %copy-done.1, f32[16,4,16]{2,0,1:T(8,128)S(1)} %get-tuple-element.198, pred[16,2048]{1,0:T(8,128)(4,1)S(1)} %broadcast_compare_fusion.2), kind=kOutput, calls=%fused_computation.11.clone.1 | convolution fusion | flops 547356672 | bytes 11046912 | tf_op jit(solution)/shard_map/while/body/eval_jaxpr/tkgj,jkd->tkgd/dot_general | solution.py:52
  67.6 0.3 fusion.38
  68.0 1.3 collective-permute-start
  69.3 1.6 collective-permute-start.2
  70.9 2.1 collective-permute-start.3
  73.0 16.0 %collective-permute-done.1 = s32[16]{0:T(128)S(1)} collective-permute-done((s32[16]{0:T(128)S(1)}, s32[16]{0:T(128)S(1)}, u32[]{:S(2)}, u32[]{:S(2)}) %collective-permute-start.1) | collective-permute-done | bytes 96 | tf_op jit(solution)/shard_map/while/body/eval_jaxpr/ppermute | solution.py:12
  89.1 1.0 copy.57
  90.1 1.6 fusion.35
  91.7 3.2 %copy-done.1 = f32[4,2048,16,16]{1,3,2,0:T(8,128)} copy-done((f32[4,2048,16,16]{1,3,2,0:T(8,128)}, f32[4,2048,16,16]{1,3,2,0:T(8,128)S(1)}, u32[]{:S(2)}) %copy-start.1) | copy-done | bytes 8388632 | tf_op jit(solution)/shard_map/while
  94.9 2.7 %fusion.36 = f32[16,4,16]{2,0,1:T(8,128)S(1)} fusion(f32[4,2048,16,16]{1,3,2,0:T(8,128)S(1)} %get-tuple-element.197, f32[16,4,16]{2,0,1:T(8,128)S(1)} %get-tuple-element.198, pred[16,2048]{1,0:T(8,128)(4,1)S(1)} %broadcast_compare_fusion.2), kind=kLoop, calls=%fused_computation.5.clone.1 | loop fusion | flops 10484736 | bytes 8429568 | tf_op jit(solution)/shard_map/while/body/eval_jaxpr/reduce_sum | solution.py:51
  97.9 5.5 %fusion.37 = f32[16,4,16,128]{3,2,0,1:T(8,128)S(1)} fusion(bf16[2048,4,128]{2,0,1:T(8,128)(2,1)} %get-tuple-element.230, f32[4,2048,16,16]{1,3,2,0:T(8,128)} %copy-done.1, f32[16,4,16]{2,0,1:T(8,128)S(1)} %get-tuple-element.198, pred[16,2048]{1,0:T(8,128)(4,1)S(1)} %broadcast_compare_fusion.2), kind=kOutput, calls=%fused_computation.11.clone.1 | convolution fusion | flops 547356672 | bytes 11046912 | tf_op jit(solution)/shard_map/while/body/eval_jaxpr/tkgj,jkd->tkgd/dot_general | solution.py:52
  103.4 0.3 fusion.38
  103.9 0.7 collective-permute-start.2
  104.6 4.2 %collective-permute-start.3 = (f32[16,64]{1,0:T(8,128)S(1)}, f32[16,64]{1,0:T(8,128)S(1)}, u32[]{:S(2)}, u32[]{:S(2)}) collective-permute-start(f32[16,64]{1,0:T(8,128)S(1)} %get-tuple-element.200), channel_id=1, source_target_pairs={{0,4},{4,8},{8,12},{12,0},{1,5},{5,9},{9,13},{13,1},{2,6},{6,10},{... | collective-permute-start | bytes 12296 | tf_op jit(solution)/shard_map/while/body/eval_jaxpr/ppermute | solution.py:12
  108.8 15.1 %collective-permute-done.1 = s32[16]{0:T(128)S(1)} collective-permute-done((s32[16]{0:T(128)S(1)}, s32[16]{0:T(128)S(1)}, u32[]{:S(2)}, u32[]{:S(2)}) %collective-permute-start.1) | collective-permute-done | bytes 96 | tf_op jit(solution)/shard_map/while/body/eval_jaxpr/ppermute | solution.py:12
  124.0 1.0 copy.57
  125.0 1.6 fusion.35
  126.7 3.2 %copy-done.1 = f32[4,2048,16,16]{1,3,2,0:T(8,128)} copy-done((f32[4,2048,16,16]{1,3,2,0:T(8,128)}, f32[4,2048,16,16]{1,3,2,0:T(8,128)S(1)}, u32[]{:S(2)}) %copy-start.1) | copy-done | bytes 8388632 | tf_op jit(solution)/shard_map/while
  129.9 2.7 %fusion.36 = f32[16,4,16]{2,0,1:T(8,128)S(1)} fusion(f32[4,2048,16,16]{1,3,2,0:T(8,128)S(1)} %get-tuple-element.197, f32[16,4,16]{2,0,1:T(8,128)S(1)} %get-tuple-element.198, pred[16,2048]{1,0:T(8,128)(4,1)S(1)} %broadcast_compare_fusion.2), kind=kLoop, calls=%fused_computation.5.clone.1 | loop fusion | flops 10484736 | bytes 8429568 | tf_op jit(solution)/shard_map/while/body/eval_jaxpr/reduce_sum | solution.py:51
  132.8 5.5 %fusion.37 = f32[16,4,16,128]{3,2,0,1:T(8,128)S(1)} fusion(bf16[2048,4,128]{2,0,1:T(8,128)(2,1)} %get-tuple-element.230, f32[4,2048,16,16]{1,3,2,0:T(8,128)} %copy-done.1, f32[16,4,16]{2,0,1:T(8,128)S(1)} %get-tuple-element.198, pred[16,2048]{1,0:T(8,128)(4,1)S(1)} %broadcast_compare_fusion.2), kind=kOutput, calls=%fused_computation.11.clone.1 | convolution fusion | flops 547356672 | bytes 11046912 | tf_op jit(solution)/shard_map/while/body/eval_jaxpr/tkgj,jkd->tkgd/dot_general | solution.py:52
  138.8 0.5 collective-permute-start.2
  139.4 4.3 %collective-permute-start.3 = (f32[16,64]{1,0:T(8,128)S(1)}, f32[16,64]{1,0:T(8,128)S(1)}, u32[]{:S(2)}, u32[]{:S(2)}) collective-permute-start(f32[16,64]{1,0:T(8,128)S(1)} %get-tuple-element.200), channel_id=1, source_target_pairs={{0,4},{4,8},{8,12},{12,0},{1,5},{5,9},{9,13},{13,1},{2,6},{6,10},{... | collective-permute-start | bytes 12296 | tf_op jit(solution)/shard_map/while/body/eval_jaxpr/ppermute | solution.py:12
  143.8 14.3 %collective-permute-done.1 = s32[16]{0:T(128)S(1)} collective-permute-done((s32[16]{0:T(128)S(1)}, s32[16]{0:T(128)S(1)}, u32[]{:S(2)}, u32[]{:S(2)}) %collective-permute-start.1) | collective-permute-done | bytes 96 | tf_op jit(solution)/shard_map/while/body/eval_jaxpr/ppermute | solution.py:12
  158.3 0.9 copy.41
  159.2 26.8 %all-gather.2.cloned.1.call-done = bf16[128,8192]{1,0:T(8,128)(2,1)} async-done(((bf16[16,8192]{1,0:T(8,128)(2,1)}), bf16[128,8192]{1,0:T(8,128)(2,1)}) %all-gather.2.cloned.1.call-update) | async-done | bytes 2097168 | tf_op jit(solution)/shard_map/all_gather | solution.py:92
  186.0 16.7 %fusion.23 = f32[128,2048]{1,0:T(8,128)} fusion(bf16[128,8192]{1,0:T(8,128)(2,1)} %all-gather.2.cloned.1.call-done, bf16[8192,2048]{1,0:T(8,128)(2,1)} %param.17), kind=kOutput, calls=%fused_computation.29 | convolution fusion | flops 4294967296 | bytes 36700160 | tf_op jit(solution)/shard_map/dot_general | solution.py:91
  202.7 19.9 %reduce-scatter.2.cloned.1.call-done = f32[64,2048]{1,0:T(8,128)} async-done(((f32[128,2048]{1,0:T(8,128)}), f32[64,2048]{1,0:T(8,128)}) %reduce-scatter.2.cloned.1.call-update) | async-done | bytes 524304 | tf_op jit(solution)/shard_map/reduce_scatter | solution.py:96
  222.6 1.8 convert_element_type.14
  (82 shorter events, 2.9 us)
Async XLA Ops:
  6.5 1.7 copy-start
  6.5 8.8 %copy-start.2 = (bf16[16,4,128]{2,1,0:T(4,128)(2,1)S(1)}, bf16[16,4,128]{2,1,0:T(4,128)(2,1)}, u32[]{:S(2)}) copy-start(bf16[16,4,128]{2,1,0:T(4,128)(2,1)} %param.14) | copy-start | bytes 49156
  6.5 8.8 %copy-start.3 = (s32[16]{0:T(128)S(1)}, s32[16]{0:T(128)}, u32[]{:S(2)}) copy-start(s32[16]{0:T(128)} %param.15) | copy-start | bytes 196
  6.5 179.5 %all-gather.2.cloned.1.call-start = ((), (), s32[]{:S(2)}) async-start(), calls=%async_computation.1 | async-start | bytes 2359296 | tf_op jit(solution)/shard_map/all_gather | solution.py:92
  18.1 3.2 %copy-start.1 = (f32[4,2048,16,16]{1,3,2,0:T(8,128)}, f32[4,2048,16,16]{1,3,2,0:T(8,128)S(1)}, u32[]{:S(2)}) copy-start(f32[4,2048,16,16]{1,3,2,0:T(8,128)S(1)} %get-tuple-element.197) | copy-start | bytes 25165828 | tf_op jit(solution)/shard_map/while
  30.1 23.1 %collective-permute-start.4 = (f32[16,64,128]{2,1,0:T(8,128)S(1)}, f32[16,64,128]{2,1,0:T(8,128)S(1)}, u32[]{:S(2)}, u32[]{:S(2)}) collective-permute-start(f32[16,64,128]{2,1,0:T(8,128)S(1)} %fusion.38), channel_id=1, source_target_pairs={{0,4},{4,8},{8,12},{12,0},{1,5},{5,9},{9,13},{13,1},{2,6},{6,10},{... | collective-permute-start | bytes 1572872 | tf_op jit(solution)/shard_map/while/body/eval_jaxpr/ppermute | solution.py:12
  33.2 20.0 %collective-permute-start = (bf16[16,64,128]{2,1,0:T(8,128)(2,1)S(1)}, bf16[16,64,128]{2,1,0:T(8,128)(2,1)}, u32[]{:S(2)}, u32[]{:S(2)}) collective-permute-start(bf16[16,64,128]{2,1,0:T(8,128)(2,1)S(1)} %copy.57), channel_id=1, source_target_pairs={{0,4},{4,8},{8,12},{12,0},{1,5},{5,9},{9,13},{13,1},{2,6},{6,10},{... | collective-permute-start | bytes 786440 | tf_op jit(solution)/shard_map/while/body/eval_jaxpr/ppermute | solution.py:12
  34.8 18.4 %collective-permute-start.2 = (f32[16,64]{1,0:T(8,128)S(1)}, f32[16,64]{1,0:T(8,128)S(1)}, u32[]{:S(2)}, u32[]{:S(2)}) collective-permute-start(f32[16,64]{1,0:T(8,128)S(1)} %get-tuple-element.199), channel_id=1, source_target_pairs={{0,4},{4,8},{8,12},{12,0},{1,5},{5,9},{9,13},{13,1},{2,6},{6,10},{... | collective-permute-start | bytes 12296 | tf_op jit(solution)/shard_map/while/body/eval_jaxpr/ppermute | solution.py:12
  36.4 16.9 %collective-permute-start.3 = (f32[16,64]{1,0:T(8,128)S(1)}, f32[16,64]{1,0:T(8,128)S(1)}, u32[]{:S(2)}, u32[]{:S(2)}) collective-permute-start(f32[16,64]{1,0:T(8,128)S(1)} %get-tuple-element.200), channel_id=1, source_target_pairs={{0,4},{4,8},{8,12},{12,0},{1,5},{5,9},{9,13},{13,1},{2,6},{6,10},{... | collective-permute-start | bytes 12296 | tf_op jit(solution)/shard_map/while/body/eval_jaxpr/ppermute | solution.py:12
  36.4 16.8 %collective-permute-start.1 = (s32[16]{0:T(128)S(1)}, s32[16]{0:T(128)S(1)}, u32[]{:S(2)}, u32[]{:S(2)}) collective-permute-start(s32[16]{0:T(128)S(1)} %copy.58), channel_id=1, source_target_pairs={{0,4},{4,8},{8,12},{12,0},{1,5},{5,9},{9,13},{13,1},{2,6},{6,10},{... | collective-permute-start | bytes 200 | tf_op jit(solution)/shard_map/while/body/eval_jaxpr/ppermute | solution.py:12
  55.9 3.2 %copy-start.1 = (f32[4,2048,16,16]{1,3,2,0:T(8,128)}, f32[4,2048,16,16]{1,3,2,0:T(8,128)S(1)}, u32[]{:S(2)}) copy-start(f32[4,2048,16,16]{1,3,2,0:T(8,128)S(1)} %get-tuple-element.197) | copy-start | bytes 25165828 | tf_op jit(solution)/shard_map/while
  68.0 21.0 %collective-permute-start.4 = (f32[16,64,128]{2,1,0:T(8,128)S(1)}, f32[16,64,128]{2,1,0:T(8,128)S(1)}, u32[]{:S(2)}, u32[]{:S(2)}) collective-permute-start(f32[16,64,128]{2,1,0:T(8,128)S(1)} %fusion.38), channel_id=1, source_target_pairs={{0,4},{4,8},{8,12},{12,0},{1,5},{5,9},{9,13},{13,1},{2,6},{6,10},{... | collective-permute-start | bytes 1572872 | tf_op jit(solution)/shard_map/while/body/eval_jaxpr/ppermute | solution.py:12
  68.0 21.0 %collective-permute-start = (bf16[16,64,128]{2,1,0:T(8,128)(2,1)S(1)}, bf16[16,64,128]{2,1,0:T(8,128)(2,1)}, u32[]{:S(2)}, u32[]{:S(2)}) collective-permute-start(bf16[16,64,128]{2,1,0:T(8,128)(2,1)S(1)} %copy.57), channel_id=1, source_target_pairs={{0,4},{4,8},{8,12},{12,0},{1,5},{5,9},{9,13},{13,1},{2,6},{6,10},{... | collective-permute-start | bytes 786440 | tf_op jit(solution)/shard_map/while/body/eval_jaxpr/ppermute | solution.py:12
  69.3 19.7 %collective-permute-start.2 = (f32[16,64]{1,0:T(8,128)S(1)}, f32[16,64]{1,0:T(8,128)S(1)}, u32[]{:S(2)}, u32[]{:S(2)}) collective-permute-start(f32[16,64]{1,0:T(8,128)S(1)} %get-tuple-element.199), channel_id=1, source_target_pairs={{0,4},{4,8},{8,12},{12,0},{1,5},{5,9},{9,13},{13,1},{2,6},{6,10},{... | collective-permute-start | bytes 12296 | tf_op jit(solution)/shard_map/while/body/eval_jaxpr/ppermute | solution.py:12
  70.9 18.1 %collective-permute-start.3 = (f32[16,64]{1,0:T(8,128)S(1)}, f32[16,64]{1,0:T(8,128)S(1)}, u32[]{:S(2)}, u32[]{:S(2)}) collective-permute-start(f32[16,64]{1,0:T(8,128)S(1)} %get-tuple-element.200), channel_id=1, source_target_pairs={{0,4},{4,8},{8,12},{12,0},{1,5},{5,9},{9,13},{13,1},{2,6},{6,10},{... | collective-permute-start | bytes 12296 | tf_op jit(solution)/shard_map/while/body/eval_jaxpr/ppermute | solution.py:12
  73.0 16.0 %collective-permute-start.1 = (s32[16]{0:T(128)S(1)}, s32[16]{0:T(128)S(1)}, u32[]{:S(2)}, u32[]{:S(2)}) collective-permute-start(s32[16]{0:T(128)S(1)} %copy.58), channel_id=1, source_target_pairs={{0,4},{4,8},{8,12},{12,0},{1,5},{5,9},{9,13},{13,1},{2,6},{6,10},{... | collective-permute-start | bytes 200 | tf_op jit(solution)/shard_map/while/body/eval_jaxpr/ppermute | solution.py:12
  91.7 3.2 %copy-start.1 = (f32[4,2048,16,16]{1,3,2,0:T(8,128)}, f32[4,2048,16,16]{1,3,2,0:T(8,128)S(1)}, u32[]{:S(2)}) copy-start(f32[4,2048,16,16]{1,3,2,0:T(8,128)S(1)} %get-tuple-element.197) | copy-start | bytes 25165828 | tf_op jit(solution)/shard_map/while
  103.7 20.2 %collective-permute-start.4 = (f32[16,64,128]{2,1,0:T(8,128)S(1)}, f32[16,64,128]{2,1,0:T(8,128)S(1)}, u32[]{:S(2)}, u32[]{:S(2)}) collective-permute-start(f32[16,64,128]{2,1,0:T(8,128)S(1)} %fusion.38), channel_id=1, source_target_pairs={{0,4},{4,8},{8,12},{12,0},{1,5},{5,9},{9,13},{13,1},{2,6},{6,10},{... | collective-permute-start | bytes 1572872 | tf_op jit(solution)/shard_map/while/body/eval_jaxpr/ppermute | solution.py:12
  103.8 20.1 %collective-permute-start = (bf16[16,64,128]{2,1,0:T(8,128)(2,1)S(1)}, bf16[16,64,128]{2,1,0:T(8,128)(2,1)}, u32[]{:S(2)}, u32[]{:S(2)}) collective-permute-start(bf16[16,64,128]{2,1,0:T(8,128)(2,1)S(1)} %copy.57), channel_id=1, source_target_pairs={{0,4},{4,8},{8,12},{12,0},{1,5},{5,9},{9,13},{13,1},{2,6},{6,10},{... | collective-permute-start | bytes 786440 | tf_op jit(solution)/shard_map/while/body/eval_jaxpr/ppermute | solution.py:12
  103.9 20.1 %collective-permute-start.2 = (f32[16,64]{1,0:T(8,128)S(1)}, f32[16,64]{1,0:T(8,128)S(1)}, u32[]{:S(2)}, u32[]{:S(2)}) collective-permute-start(f32[16,64]{1,0:T(8,128)S(1)} %get-tuple-element.199), channel_id=1, source_target_pairs={{0,4},{4,8},{8,12},{12,0},{1,5},{5,9},{9,13},{13,1},{2,6},{6,10},{... | collective-permute-start | bytes 12296 | tf_op jit(solution)/shard_map/while/body/eval_jaxpr/ppermute | solution.py:12
  104.6 19.4 %collective-permute-start.3 = (f32[16,64]{1,0:T(8,128)S(1)}, f32[16,64]{1,0:T(8,128)S(1)}, u32[]{:S(2)}, u32[]{:S(2)}) collective-permute-start(f32[16,64]{1,0:T(8,128)S(1)} %get-tuple-element.200), channel_id=1, source_target_pairs={{0,4},{4,8},{8,12},{12,0},{1,5},{5,9},{9,13},{13,1},{2,6},{6,10},{... | collective-permute-start | bytes 12296 | tf_op jit(solution)/shard_map/while/body/eval_jaxpr/ppermute | solution.py:12
  108.8 15.2 %collective-permute-start.1 = (s32[16]{0:T(128)S(1)}, s32[16]{0:T(128)S(1)}, u32[]{:S(2)}, u32[]{:S(2)}) collective-permute-start(s32[16]{0:T(128)S(1)} %copy.58), channel_id=1, source_target_pairs={{0,4},{4,8},{8,12},{12,0},{1,5},{5,9},{9,13},{13,1},{2,6},{6,10},{... | collective-permute-start | bytes 200 | tf_op jit(solution)/shard_map/while/body/eval_jaxpr/ppermute | solution.py:12
  126.7 3.2 %copy-start.1 = (f32[4,2048,16,16]{1,3,2,0:T(8,128)}, f32[4,2048,16,16]{1,3,2,0:T(8,128)S(1)}, u32[]{:S(2)}) copy-start(f32[4,2048,16,16]{1,3,2,0:T(8,128)S(1)} %get-tuple-element.197) | copy-start | bytes 25165828 | tf_op jit(solution)/shard_map/while
  138.7 19.4 %collective-permute-start.4 = (f32[16,64,128]{2,1,0:T(8,128)S(1)}, f32[16,64,128]{2,1,0:T(8,128)S(1)}, u32[]{:S(2)}, u32[]{:S(2)}) collective-permute-start(f32[16,64,128]{2,1,0:T(8,128)S(1)} %fusion.38), channel_id=1, source_target_pairs={{0,4},{4,8},{8,12},{12,0},{1,5},{5,9},{9,13},{13,1},{2,6},{6,10},{... | collective-permute-start | bytes 1572872 | tf_op jit(solution)/shard_map/while/body/eval_jaxpr/ppermute | solution.py:12
  138.7 19.3 %collective-permute-start = (bf16[16,64,128]{2,1,0:T(8,128)(2,1)S(1)}, bf16[16,64,128]{2,1,0:T(8,128)(2,1)}, u32[]{:S(2)}, u32[]{:S(2)}) collective-permute-start(bf16[16,64,128]{2,1,0:T(8,128)(2,1)S(1)} %copy.57), channel_id=1, source_target_pairs={{0,4},{4,8},{8,12},{12,0},{1,5},{5,9},{9,13},{13,1},{2,6},{6,10},{... | collective-permute-start | bytes 786440 | tf_op jit(solution)/shard_map/while/body/eval_jaxpr/ppermute | solution.py:12
  138.8 19.2 %collective-permute-start.2 = (f32[16,64]{1,0:T(8,128)S(1)}, f32[16,64]{1,0:T(8,128)S(1)}, u32[]{:S(2)}, u32[]{:S(2)}) collective-permute-start(f32[16,64]{1,0:T(8,128)S(1)} %get-tuple-element.199), channel_id=1, source_target_pairs={{0,4},{4,8},{8,12},{12,0},{1,5},{5,9},{9,13},{13,1},{2,6},{6,10},{... | collective-permute-start | bytes 12296 | tf_op jit(solution)/shard_map/while/body/eval_jaxpr/ppermute | solution.py:12
  139.4 18.7 %collective-permute-start.3 = (f32[16,64]{1,0:T(8,128)S(1)}, f32[16,64]{1,0:T(8,128)S(1)}, u32[]{:S(2)}, u32[]{:S(2)}) collective-permute-start(f32[16,64]{1,0:T(8,128)S(1)} %get-tuple-element.200), channel_id=1, source_target_pairs={{0,4},{4,8},{8,12},{12,0},{1,5},{5,9},{9,13},{13,1},{2,6},{6,10},{... | collective-permute-start | bytes 12296 | tf_op jit(solution)/shard_map/while/body/eval_jaxpr/ppermute | solution.py:12
  143.7 14.4 %collective-permute-start.1 = (s32[16]{0:T(128)S(1)}, s32[16]{0:T(128)S(1)}, u32[]{:S(2)}, u32[]{:S(2)}) collective-permute-start(s32[16]{0:T(128)S(1)} %copy.58), channel_id=1, source_target_pairs={{0,4},{4,8},{8,12},{12,0},{1,5},{5,9},{9,13},{13,1},{2,6},{6,10},{... | collective-permute-start | bytes 200 | tf_op jit(solution)/shard_map/while/body/eval_jaxpr/ppermute | solution.py:12
  159.2 63.4 %reduce-scatter.2.cloned.1.call-start = ((), (), s32[]{:S(2)}) async-start(), calls=%async_computation.2 | async-start | bytes 1572864 | tf_op jit(solution)/shard_map/reduce_scatter | solution.py:96
Sparse Core Ops, SparseCore 0:
  159.3 26.6 all-gather.1
  202.8 19.7 reduce-scatter.1
where the time goes:
time: 232 us; the launch traced here: 231 us
  waiting for transfers between devices  107 us (46%)
  matrix products  46.1 us (20%)
  local copies, waits for them, and re-layouts  25.4 us (11%)
  starting transfers between devices  23.3 us (10%)
  other arithmetic  14.7 us (6%)
  between operations  14.1 us (6%)
    ppermute x20, waiting for transfers between devices, shifted(): return lax.ppermute(value, axis, pairs)  60.5 us
    all_gather x1, waiting for transfers between devices, local(): lax.all_gather(attended, ('ctx', 'rep'), axis=0, tiled=True)  26.8 us
    ppermute x20, starting transfers between devices, shifted(): return lax.ppermute(value, axis, pairs)  23.2 us
    dot_general x4, matrix products, attend(): jnp.einsum('tkgj,jkd->tkgd', weights.astype(jnp.bfloat16), cache_values,...  21.8 us
    reduce_scatter x1, waiting for transfers between devices, local(): lax.psum_scatter(terms, 'heads', scatter_dimension=0, tiled=True)  19.9 us
    dot_general x1, matrix products, local(): jnp.dot(lax.all_gather(attended, ('ctx', 'rep'), axis=0, tiled=True), out...  16.7 us
    while x16, local copies, waits for them, and re-layouts  16.6 us
    reduce_sum x4, other arithmetic, attend(): totals = jnp.sum(weights, axis=-1)  10.9 us
  transfers between devices with their start and end apart: 22, of which 6 were waited for; matrix products, arithmetic and copies ran while one was open for 0% of the time, Pallas kernels for 0%

commit v1 on v0

v1 whole, which is shorter than its diff:
```python
import functools

import jax
import jax.numpy as jnp
from jax import lax
from jax.experimental import pallas as pl
from jax.experimental.pallas import tpu as pltpu
from jax.sharding import PartitionSpec as P

MASKED = -1e30
FLOOR = -1e29
LOG2E = 1.4426950408889634
MESH = pl.DeviceIdType.MESH
NT = (((1,), (1,)), ((), ()))


def kernel(
    sizes, q_ref, lim_ref, key_ref, val_ref, nk_ref, nv_ref, w_ref, out_ref,
    qg, limg, scores, psend, precv, ssend, srecv, att, acc, xsend, xrecv, wbuf,
    q_ss, q_rs, l_ss, l_rs, p_ss, p_rs, s_ss, s_rs, a_ss, a_rs, c_ss, c_rs, x_ss, x_rs, w_sem,
):
    n_ctx, n_rep, n_heads, kv, rows, per_group, head, block = sizes
    z, r, x = lax.axis_index("ctx"), lax.axis_index("rep"), lax.axis_index("heads")
    lanes = per_group * rows
    factor = head ** (-0.5) * LOG2E
    piece = min(512, block)
    depth = per_group * head
    columns = w_ref.shape[1]
    tile = min(512, columns)
    out_rows = out_ref.shape[0]

    def w_copy(k):
        return pltpu.make_async_copy(w_ref.at[pl.ds(pl.multiple_of(k * depth, depth), depth), :], wbuf.at[k], w_sem.at[k])

    def remote(src, dst, send, recv, **where):
        return pltpu.make_async_remote_copy(
            src_ref=src, dst_ref=dst, send_sem=send, recv_sem=recv, device_id=where, device_id_type=MESH
        )

    def q_copy(k, s, way):
        return remote(qg.at[k, s], qg.at[k, s], q_ss.at[k, s, way], q_rs.at[k, s], ctx=z + 1 - 2 * way)

    def lim_copy(s, d):
        return remote(limg.at[s], limg.at[s], l_ss.at[d], l_rs.at[s], ctx=d)

    def p_copy(k, s):
        return remote(psend.at[k, s], precv.at[k, z], p_ss.at[k, s], p_rs.at[k, z], ctx=s)

    def p_arrival(k, s):
        return remote(psend.at[k, s], precv.at[k, s], p_ss.at[k, s], p_rs.at[k, s], ctx=s)

    def s_copy(k, s):
        return remote(ssend.at[k, s], srecv.at[k, z], s_ss.at[k, s], s_rs.at[k, z], ctx=s)

    def s_arrival(k, s):
        return remote(ssend.at[k, s], srecv.at[k, s], s_ss.at[k, s], s_rs.at[k, s], ctx=s)

    def a_copy(k, s, way):
        return remote(att.at[k, s, r], att.at[k, s, r], a_ss.at[k, s, way], a_rs.at[k, s], ctx=z + 1 - 2 * way)

    def c_copy(k, s, step):
        other = lax.rem(r + step, n_rep)
        return remote(att.at[k, s, r], att.at[k, s, r], c_ss.at[k, s, step - 1], c_rs.at[k, s, r], rep=other)

    def c_arrival(k, s, step):
        other = lax.rem(r + step, n_rep)
        return remote(att.at[k, s, other], att.at[k, s, other], c_ss.at[k, s, step - 1], c_rs.at[k, s, other], rep=other)

    def x_copy(t, other):
        cols = pl.ds(t * tile, tile)
        return remote(xsend.at[other, :, cols], xrecv.at[x, :, cols], x_ss.at[t, other], x_rs.at[t, x], heads=other)

    def x_arrival(t, other):
        cols = pl.ds(t * tile, tile)
        return remote(xsend.at[other, :, cols], xrecv.at[other, :, cols], x_ss.at[t, other], x_rs.at[t, other], heads=other)

    for k in range(kv):
        w_copy(k).start()

    barrier = pltpu.get_barrier_semaphore()
    for step in range(1, n_ctx):
        pl.semaphore_signal(barrier, inc=1, device_id={"ctx": lax.rem(z + step, n_ctx)}, device_id_type=MESH)
    for step in range(1, n_rep):
        pl.semaphore_signal(barrier, inc=1, device_id={"rep": lax.rem(r + step, n_rep)}, device_id_type=MESH)
    for step in range(1, n_heads):
        pl.semaphore_signal(barrier, inc=1, device_id={"heads": lax.rem(x + step, n_heads)}, device_id_type=MESH)
    qg[:, z] = q_ref[...]
    limg[z] = lim_ref[...]
    pl.semaphore_wait(barrier, n_ctx + n_rep + n_heads - 3)

    right, left = z < n_ctx - 1, z > 0

    def send_own(k):
        @pl.when(right)
        def _():
            q_copy(k, z, 0).start()

        @pl.when(left)
        def _():
            q_copy(k, z, 1).start()

    send_own(0)
    for step in range(1, n_ctx):
        lim_copy(z, lax.rem(z + step, n_ctx)).start()

    def attend(k, s):
        query = qg[k, s]
        limit = limg[s][0:1, :] - z * block
        peak = jnp.full((1, lanes), FLOOR, jnp.float32)
        for c in range(block // piece):
            span = slice(c * piece, (c + 1) * piece)
            raw = lax.dot_general(key_ref[k, span, :], query, NT, preferred_element_type=jnp.float32)
            slot = lax.broadcasted_iota(jnp.int32, (piece, lanes), 0) + c * piece
            raw = jnp.where(slot < limit, raw, MASKED)
            scores[span, :] = raw
            peak = jnp.maximum(peak, jnp.max(raw, axis=0, keepdims=True))
        total = jnp.zeros((1, lanes), jnp.float32)
        output = jnp.zeros((head, lanes), jnp.float32)
        for c in range(block // piece):
            span = slice(c * piece, (c + 1) * piece)
            weights = jnp.exp2((scores[span, :] - peak) * factor)
            total = total + jnp.sum(weights, axis=0, keepdims=True)
            output = output + jnp.dot(val_ref[k, :, span], weights.astype(jnp.bfloat16), preferred_element_type=jnp.float32)
        row = lax.broadcasted_iota(jnp.int32, (8, lanes), 0)
        stats = jnp.where(row == 0, peak, total)

        @pl.when(s == z)
        def _():
            precv[k, z] = output.astype(jnp.bfloat16)
            srecv[k, z] = stats

        @pl.when(s != z)
        def _():
            psend[k, s] = output.astype(jnp.bfloat16)
            ssend[k, s] = stats
            p_copy(k, s).start()
            s_copy(k, s).start()

    def attention(k):
        @pl.when(k + 1 < kv)
        def _():
            send_own(k + 1)

        def visit(i, carry):
            @pl.when(jnp.logical_and(i > 0, z - i >= 0))
            def _():
                q_copy(k, z - i, 0).wait_recv()

                @pl.when(right)
                def _():
                    q_copy(k, z - i, 0).start()

                @pl.when(k == 0)
                def _():
                    lim_copy(z - i, z - i).wait_recv()

            @pl.when(jnp.logical_and(i > 0, z + i < n_ctx))
            def _():
                q_copy(k, z + i, 1).wait_recv()

                @pl.when(left)
                def _():
                    q_copy(k, z + i, 1).start()

                @pl.when(k == 0)
                def _():
                    lim_copy(z + i, z + i).wait_recv()

            def side(j, inner):
                s = z - i + 2 * i * j
                real = jnp.logical_and(s >= 0, s < n_ctx)

                @pl.when(jnp.logical_and(real, jnp.logical_or(i > 0, j == 0)))
                def _():
                    attend(k, s)

                return inner

            return lax.fori_loop(0, 2, side, carry)

        lax.fori_loop(0, n_ctx, visit, 0)

    def merge(k):
        for step in range(1, n_ctx):
            s = lax.rem(z + step, n_ctx)
            p_arrival(k, s).wait_recv()
            s_arrival(k, s).wait_recv()
        query = qg[k, z]
        own_all = lax.dot_general(nk_ref[k], query, NT, preferred_element_type=jnp.float32)
        token = lax.rem(lax.broadcasted_iota(jnp.int32, (rows, lanes), 1), rows)
        same = token == lax.broadcasted_iota(jnp.int32, (rows, lanes), 0)
        own = jnp.sum(jnp.where(same, own_all, 0.0), axis=0, keepdims=True)
        own_value = jnp.dot(
            nv_ref[k], jnp.where(same, 1.0, 0.0).astype(jnp.bfloat16), preferred_element_type=jnp.float32
        )
        top = own
        for b in range(n_ctx):
            top = jnp.maximum(top, srecv[k, b, 0:1, :])
        share = jnp.exp2((own - top) * factor)
        below = share
        above = share * own_value
        for b in range(n_ctx):
            share = jnp.exp2((srecv[k, b, 0:1, :] - top) * factor)
            below = below + share * srecv[k, b, 1:2, :]
            above = above + share * precv[k, b].astype(jnp.float32)
        result = jnp.transpose(above / below).astype(jnp.bfloat16)
        for h in range(per_group):
            att[k, z, r, :, h * head : (h + 1) * head] = result[h * rows : (h + 1) * rows, :]

        @pl.when(right)
        def _():
            a_copy(k, z, 0).start()

        @pl.when(left)
        def _():
            a_copy(k, z, 1).start()

        for step in range(1, n_rep):
            c_copy(k, z, step).start()

    def collect(k):
        def hop(i, carry):
            @pl.when(z - i >= 0)
            def _():
                a_copy(k, z - i, 0).wait_recv()

                @pl.when(right)
                def _():
                    a_copy(k, z - i, 0).start()

                for step in range(1, n_rep):
                    c_copy(k, z - i, step).start()

            @pl.when(z + i < n_ctx)
            def _():
                a_copy(k, z + i, 1).wait_recv()

                @pl.when(left)
                def _():
                    a_copy(k, z + i, 1).start()

                for step in range(1, n_rep):
                    c_copy(k, z + i, step).start()

            return carry

        lax.fori_loop(1, n_ctx, hop, 0)
        for step in range(1, n_rep):
            for s in range(n_ctx):
                c_arrival(k, s, step).wait_recv()
        w_copy(k).wait()

    def product(k, t):
        cols = pl.ds(pl.multiple_of(t * tile, tile), tile)
        term = jnp.dot(
            att[k].reshape(n_ctx * n_rep * rows, depth), wbuf[k, :, cols], preferred_element_type=jnp.float32
        )
        acc[:, cols] += term

    acc[...] = jnp.zeros_like(acc)

    def stage(k, carry):
        @pl.when(k < kv)
        def _():
            attention(k)

        @pl.when(k >= 1)
        def _():
            merge(k - 1)

        @pl.when(k >= 2)
        def _():
            collect(k - 2)
            lax.fori_loop(0, columns // tile, lambda t, c: (product(k - 2, t), c)[1], 0)

        return carry

    lax.fori_loop(0, kv + 1, stage, 0)
    collect(kv - 1)
    for t in range(columns // tile):
        product(kv - 1, t)
        for other in range(n_heads):
            xsend[other, :, t * tile : (t + 1) * tile] = acc[
                other * out_rows : (other + 1) * out_rows, t * tile : (t + 1) * tile
            ].astype(jnp.bfloat16)
        for step in range(1, n_heads):
            x_copy(t, lax.rem(x + step, n_heads)).start()
    for t in range(columns // tile):
        cols = slice(t * tile, (t + 1) * tile)
        total = acc[pl.ds(pl.multiple_of(x * out_rows, out_rows), out_rows), cols]
        for step in range(1, n_heads):
            other = lax.rem(x + step, n_heads)
            x_arrival(t, other).wait_recv()
            total = total + xrecv[other, :, cols].astype(jnp.float32)
        out_ref[:, cols] = total.astype(jnp.bfloat16)

    for step in range(1, n_ctx):
        lim_copy(z, lax.rem(z + step, n_ctx)).wait_send()

    def drain(k, carry):
        def each(s, inner):
            @pl.when(s != z)
            def _():
                p_copy(k, s).wait_send()
                s_copy(k, s).wait_send()

            @pl.when(jnp.logical_and(right, s <= z))
            def _():
                q_copy(k, s, 0).wait_send()
                a_copy(k, s, 0).wait_send()

            @pl.when(jnp.logical_and(left, s >= z))
            def _():
                q_copy(k, s, 1).wait_send()
                a_copy(k, s, 1).wait_send()

            for step in range(1, n_rep):
                c_copy(k, s, step).wait_send()
            return inner

        return lax.fori_loop(0, n_ctx, each, carry)

    lax.fori_loop(0, kv, drain, 0)
    for t in range(columns // tile):
        for step in range(1, n_heads):
            x_copy(t, lax.rem(x + step, n_heads)).wait_send()


def local(mesh_shape, queries, cache_keys, cache_values, new_keys, new_values, positions, cached_length, out_weight):
    rows, local_heads, head = queries.shape
    block, kv = cache_keys.shape[0], cache_keys.shape[1]
    per_group = local_heads // kv
    n_ctx, n_rep, n_heads = mesh_shape["ctx"], mesh_shape["rep"], mesh_shape["heads"]
    lanes = per_group * rows
    depth = per_group * head
    columns = out_weight.shape[1]
    tile = min(512, columns)
    tokens = n_ctx * n_rep * rows
    out_rows = tokens // n_heads

    grouped = queries.reshape(rows, kv, per_group, head).transpose(1, 2, 0, 3).reshape(kv, lanes, head)
    limits = jnp.minimum(cached_length[0], positions)
    limits = jnp.broadcast_to(limits[None, None, :], (8, per_group, rows)).reshape(8, lanes)
    keys = cache_keys.transpose(1, 0, 2)
    values = cache_values.transpose(1, 2, 0)
    own_keys = new_keys.transpose(1, 0, 2)
    own_values = new_values.transpose(1, 2, 0)

    sizes = (n_ctx, n_rep, n_heads, kv, rows, per_group, head, block)
    dma = pltpu.SemaphoreType.DMA
    vmem = pl.BlockSpec(memory_space=pltpu.VMEM)
    return pl.pallas_call(
        functools.partial(kernel, sizes),
        out_shape=jax.ShapeDtypeStruct((out_rows, columns), jnp.bfloat16),
        in_specs=[vmem] * 6 + [pl.BlockSpec(memory_space=pl.ANY)],
        out_specs=vmem,
        scratch_shapes=[
            pltpu.VMEM((kv, n_ctx, lanes, head), jnp.bfloat16),
            pltpu.VMEM((n_ctx, 8, lanes), jnp.int32),
            pltpu.VMEM((block, lanes), jnp.float32),
            pltpu.VMEM((kv, n_ctx, head, lanes), jnp.bfloat16),
            pltpu.VMEM((kv, n_ctx, head, lanes), jnp.bfloat16),
            pltpu.VMEM((kv, n_ctx, 8, lanes), jnp.float32),
            pltpu.VMEM((kv, n_ctx, 8, lanes), jnp.float32),
            pltpu.VMEM((kv, n_ctx, n_rep, rows, depth), jnp.bfloat16),
            pltpu.VMEM((tokens, columns), jnp.float32),
            pltpu.VMEM((n_heads, out_rows, columns), jnp.bfloat16),
            pltpu.VMEM((n_heads, out_rows, columns), jnp.bfloat16),
            pltpu.VMEM((kv, depth, columns), jnp.bfloat16),
            dma((kv, n_ctx, 2)),
            dma((kv, n_ctx)),
            dma((n_ctx,)),
            dma((n_ctx,)),
            dma((kv, n_ctx)),
            dma((kv, n_ctx)),
            dma((kv, n_ctx)),
            dma((kv, n_ctx)),
            dma((kv, n_ctx, 2)),
            dma((kv, n_ctx)),
            dma((kv, n_ctx, n_rep)),
            dma((kv, n_ctx, n_rep)),
            dma((columns // tile, n_heads)),
            dma((columns // tile, n_heads)),
            dma((kv,)),
        ],
        compiler_params=pltpu.CompilerParams(
            collective_id=0, has_side_effects=True, vmem_limit_bytes=60 * 1024 * 1024
        ),
    )(grouped, limits, keys, values, own_keys, own_values, out_weight)


def solution(mesh):
    return jax.shard_map(
        functools.partial(local, dict(mesh.shape)),
        mesh=mesh,
        in_specs=(
            P(("groups", "ctx", "rep"), "heads", None),
            P(("groups", "ctx"), "heads", None),
            P(("groups", "ctx"), "heads", None),
            P(("groups", "ctx", "rep"), "heads", None),
            P(("groups", "ctx", "rep"), "heads", None),
            P(("groups", "ctx", "rep")),
            P("groups"),
            P("heads", ("ctx", "rep")),
        ),
        out_specs=P(("groups", "heads"), ("ctx", "rep")),
        check_vma=False,
    )
```

time: 232 us -> 106 us (0.46)
  waiting for transfers between devices: 107 us -> 0 us
  Pallas kernels: 0 us -> 90.9 us
  matrix products: 46.1 us -> 0 us
  starting transfers between devices: 23.3 us -> 0 us
  other arithmetic: 14.7 us -> 0.66 us
  between operations: 14.1 us -> 0.67 us
  local copies, waits for them, and re-layouts: 25.4 us -> 13 us
    pallas_call x0 -> x1, Pallas kernels: none -> 90.9 us  [local(): pl.pallas_call(functools.partial(kernel, sizes), out_shape=jax.ShapeDtype...]
    ppermute x20 -> x0, waiting for transfers between devices: 60.5 us -> none  [shifted(): return lax.ppermute(value, axis, pairs)]
    dot_general x10 -> x0, matrix products: 46.1 us -> none  [the longest x4 21.8 us: attend(): jnp.einsum('tkgj,jkd->tkgd', weights.astype(jnp.bfloat16), cache_values,...]
    all_gather x1 -> x0, waiting for transfers between devices: 26.8 us -> none  [local(): lax.all_gather(attended, ('ctx', 'rep'), axis=0, tiled=True)]
    ppermute x20 -> x0, starting transfers between devices: 23.2 us -> none  [shifted(): return lax.ppermute(value, axis, pairs)]
    reduce_scatter x1 -> x0, waiting for transfers between devices: 19.9 us -> none  [local(): lax.psum_scatter(terms, 'heads', scatter_dimension=0, tiled=True)]
    while x16 -> x0, local copies, waits for them, and re-layouts: 16.6 us -> none
    reduce_sum x4 -> x0, other arithmetic: 10.9 us -> none  [attend(): totals = jnp.sum(weights, axis=-1)]
  transfers between devices with their start and end apart: 22 -> 0, of which waited for: 6 -> 0; matrix products, arithmetic and copies ran while one was open for 0% -> 0% of each run, Pallas kernels for 0% -> 0%
where the time goes in v1:
time: 106 us; the launch traced here: 105 us
  Pallas kernels  90.9 us (86%)
  local copies, waits for them, and re-layouts  13 us (12%)
    pallas_call x1, Pallas kernels, local(): pl.pallas_call(functools.partial(kernel, sizes), out_shape=jax.ShapeDtype...  90.9 us
    unnamed x7, local copies, waits for them, and re-layouts  10.5 us

profile of v1, /device:TPU:0, one launch (start us, length us, event | category | flops | bytes accessed | tf_op | source)
XLA Modules:
  0.0 105.2 jit_solution(11829603597025964760)
XLA Ops:
  0.7 0.7 broadcast_minimum_fusion
  1.3 0.1 broadcast_in_dim.11
  1.4 0.6 broadcast_in_dim.12.lim_ref
  2.0 1.3 %copy.17 = bf16[16,4,128]{2,0,1:T(8,128)(2,1)} copy(bf16[16,4,128]{2,1,0:T(4,128)(2,1)} %param.11) | data formatting | bytes 32768 | tf_op args[3]
  3.3 1.5 %copy.13 = bf16[16,4,128]{0,2,1:T(8,128)(2,1)} copy(bf16[16,4,128]{2,1,0:T(4,128)(2,1)} %param.12) | data formatting | bytes 32768 | tf_op args[4]
  4.8 1.8 %copy.9 = bf16[16,4,16,128]{3,0,2,1:T(8,128)(2,1)} copy(bf16[16,4,16,128]{3,2,1,0:T(8,128)(2,1)} %bitcast.18) | data formatting | bytes 524288 | tf_op jit(solution)/shard_map/reshape | solution.py:341
  6.6 0.0 copy-start
  6.6 3.4 %copy.16 = bf16[2048,4,128]{2,0,1:T(8,128)(2,1)} copy(bf16[2048,4,128]{2,1,0:T(4,128)(2,1)} %param.9) | data formatting | bytes 4194304 | tf_op args[1]
  10.0 0.0 copy-done
  10.0 2.7 %copy.11 = bf16[2048,4,128]{0,2,1:T(8,128)(2,1)} copy(bf16[2048,4,128]{2,1,0:T(4,128)(2,1)S(1)} %copy-done) | data formatting | bytes 4194304 | tf_op args[2]
  12.7 90.9 %shard_map.82 = bf16[64,2048]{1,0:T(8,128)(2,1)} custom-call(bf16[4,256,128]{2,1,0:T(8,128)(2,1)} %bitcast.16, s32[8,256]{1,0:T(8,128)} %broadcast_in_dim.12.lim_ref, bf16[4,2048,128]{2,1,0:T(8,128)(2,1)} %bitcast.14, bf16[4,128,2048]{2,1,0:T(8,128)(2,1)} %bitcast.15, bf16[4,16,128]{2,1,0:T(8,128)(2,1)} %bitcast.19, bf16[4,128,16]{2,1,0:T(8,128)(2,1)} %bitcast.17, ...), custom_call_target="tpu_custom_call" | custom-call | tf_op jit(solution)/shard_map/pallas_call | solution.py:352
  103.6 1.7 %copy.20 = bf16[64,2048]{1,0:T(8,128)(2,1)} copy(bf16[64,2048]{1,0:T(8,128)(2,1)} %shard_map.82) | data formatting | bytes 524288
  (1 shorter events, 0.0 us)
Async XLA Ops:
  6.6 3.4 %copy-start = (bf16[2048,4,128]{2,1,0:T(4,128)(2,1)S(1)}, bf16[2048,4,128]{2,1,0:T(4,128)(2,1)}, u32[]{:S(2)}) copy-start(bf16[2048,4,128]{2,1,0:T(4,128)(2,1)} %param.10) | copy-start | bytes 6291460

commit v2 on v1

--- a/solution.py
+++ b/solution.py
@@ -15,9 +15,9 @@
 
 
 def kernel(
-    sizes, q_ref, lim_ref, key_ref, val_ref, nk_ref, nv_ref, w_ref, out_ref,
-    qg, limg, scores, psend, precv, ssend, srecv, att, acc, xsend, xrecv, wbuf,
-    q_ss, q_rs, l_ss, l_rs, p_ss, p_rs, s_ss, s_rs, a_ss, a_rs, c_ss, c_rs, x_ss, x_rs, w_sem,
+    sizes, pos_ref, len_ref, q_ref, ck_ref, cv_ref, nk_ref, nv_ref, w_ref, out_ref,
+    wide, kraw, vraw, key_ref, val_ref, qg, limg, scores, psend, precv, ssend, srecv, att, acc, xsend, xrecv, wbuf,
+    q_ss, q_rs, l_ss, l_rs, p_ss, p_rs, s_ss, s_rs, a_ss, a_rs, c_ss, c_rs, x_ss, x_rs, w_sem, kv_sem,
 ):
     n_ctx, n_rep, n_heads, kv, rows, per_group, head, block = sizes
     z, r, x = lax.axis_index("ctx"), lax.axis_index("rep"), lax.axis_index("heads")
@@ -74,6 +74,10 @@
         cols = pl.ds(t * tile, tile)
         return remote(xsend.at[other, :, cols], xrecv.at[other, :, cols], x_ss.at[t, other], x_rs.at[t, other], heads=other)
 
+    k_copy = pltpu.make_async_copy(ck_ref, kraw, kv_sem.at[0])
+    v_copy = pltpu.make_async_copy(cv_ref, vraw, kv_sem.at[1])
+    k_copy.start()
+    v_copy.start()
     for k in range(kv):
         w_copy(k).start()
 
@@ -84,8 +88,17 @@
         pl.semaphore_signal(barrier, inc=1, device_id={"rep": lax.rem(r + step, n_rep)}, device_id_type=MESH)
     for step in range(1, n_heads):
         pl.semaphore_signal(barrier, inc=1, device_id={"heads": lax.rem(x + step, n_heads)}, device_id_type=MESH)
-    qg[:, z] = q_ref[...]
-    limg[z] = lim_ref[...]
+    heads_here = kv * per_group
+    wide[: rows * heads_here, :] = q_ref[...].astype(jnp.float32)
+    for k in range(kv):
+        for h in range(per_group):
+            picked = wide[pl.ds(k * per_group + h, rows, stride=heads_here), :]
+            qg[k, z, h * rows : (h + 1) * rows, :] = picked.astype(jnp.bfloat16)
+    lane_token = lax.rem(lax.broadcasted_iota(jnp.int32, (8, lanes), 1), rows)
+    limit_row = jnp.zeros((8, lanes), jnp.int32)
+    for t in range(rows):
+        limit_row = jnp.where(lane_token == t, jnp.minimum(len_ref[0], pos_ref[t]), limit_row)
+    limg[z] = limit_row
     pl.semaphore_wait(barrier, n_ctx + n_rep + n_heads - 3)
 
     right, left = z < n_ctx - 1, z > 0
@@ -102,6 +115,29 @@
     send_own(0)
     for step in range(1, n_ctx):
         lim_copy(z, lax.rem(z + step, n_ctx)).start()
+
+    batch = min(256, block)
+
+    def unpack(c, carry):
+        source = pl.ds(pl.multiple_of(c * batch * kv, batch * kv), batch * kv)
+        span = pl.ds(pl.multiple_of(c * batch, batch), batch)
+        wide[: batch * kv, :] = kraw[source, :].astype(jnp.float32)
+        for k in range(kv):
+            key_ref[k, span, :] = wide[pl.ds(k, batch, stride=kv), :].astype(jnp.bfloat16)
+        return carry
+
+    def unpack_values(c, carry):
+        source = pl.ds(pl.multiple_of(c * batch * kv, batch * kv), batch * kv)
+        span = pl.ds(pl.multiple_of(c * batch, batch), batch)
+        wide[: batch * kv, :] = vraw[source, :].astype(jnp.float32)
+        for k in range(kv):
+            val_ref[k, :, span] = jnp.transpose(wide[pl.ds(k, batch, stride=kv), :]).astype(jnp.bfloat16)
+        return carry
+
+    k_copy.wait()
+    lax.fori_loop(0, block // batch, unpack, 0)
+    v_copy.wait()
+    lax.fori_loop(0, block // batch, unpack_values, 0)
 
     def attend(k, s):
         query = qg[k, s]
@@ -186,12 +222,18 @@
             p_arrival(k, s).wait_recv()
             s_arrival(k, s).wait_recv()
         query = qg[k, z]
-        own_all = lax.dot_general(nk_ref[k], query, NT, preferred_element_type=jnp.float32)
+        wide[: rows * kv, :] = nk_ref[...].astype(jnp.float32)
+        own_key = wide[pl.ds(k, rows, stride=kv), :].astype(jnp.bfloat16)
+        own_all = lax.dot_general(own_key, query, NT, preferred_element_type=jnp.float32)
         token = lax.rem(lax.broadcasted_iota(jnp.int32, (rows, lanes), 1), rows)
         same = token == lax.broadcasted_iota(jnp.int32, (rows, lanes), 0)
         own = jnp.sum(jnp.where(same, own_all, 0.0), axis=0, keepdims=True)
-        own_value = jnp.dot(
-            nv_ref[k], jnp.where(same, 1.0, 0.0).astype(jnp.bfloat16), preferred_element_type=jnp.float32
+        wide[: rows * kv, :] = nv_ref[...].astype(jnp.float32)
+        own_value = lax.dot_general(
+            wide[pl.ds(k, rows, stride=kv), :].astype(jnp.bfloat16),
+            jnp.where(same, 1.0, 0.0).astype(jnp.bfloat16),
+            (((0,), (0,)), ((), ())),
+            preferred_element_type=jnp.float32,
         )
         top = own
         for b in range(n_ctx):
@@ -338,23 +380,22 @@
     tokens = n_ctx * n_rep * rows
     out_rows = tokens // n_heads
 
-    grouped = queries.reshape(rows, kv, per_group, head).transpose(1, 2, 0, 3).reshape(kv, lanes, head)
-    limits = jnp.minimum(cached_length[0], positions)
-    limits = jnp.broadcast_to(limits[None, None, :], (8, per_group, rows)).reshape(8, lanes)
-    keys = cache_keys.transpose(1, 0, 2)
-    values = cache_values.transpose(1, 2, 0)
-    own_keys = new_keys.transpose(1, 0, 2)
-    own_values = new_values.transpose(1, 2, 0)
-
     sizes = (n_ctx, n_rep, n_heads, kv, rows, per_group, head, block)
     dma = pltpu.SemaphoreType.DMA
     vmem = pl.BlockSpec(memory_space=pltpu.VMEM)
+    smem = pl.BlockSpec(memory_space=pltpu.SMEM)
+    anywhere = pl.BlockSpec(memory_space=pl.ANY)
     return pl.pallas_call(
         functools.partial(kernel, sizes),
         out_shape=jax.ShapeDtypeStruct((out_rows, columns), jnp.bfloat16),
-        in_specs=[vmem] * 6 + [pl.BlockSpec(memory_space=pl.ANY)],
+        in_specs=[smem, smem, vmem, anywhere, anywhere, vmem, vmem, anywhere],
         out_specs=vmem,
         scratch_shapes=[
+            pltpu.VMEM((max(rows * local_heads, min(256, block) * kv), head), jnp.float32),
+            pltpu.VMEM((block * kv, head), jnp.bfloat16),
+            pltpu.VMEM((block * kv, head), jnp.bfloat16),
+            pltpu.VMEM((kv, block, head), jnp.bfloat16),
+            pltpu.VMEM((kv, head, block), jnp.bfloat16),
             pltpu.VMEM((kv, n_ctx, lanes, head), jnp.bfloat16),
             pltpu.VMEM((n_ctx, 8, lanes), jnp.int32),
             pltpu.VMEM((block, lanes), jnp.float32),
@@ -382,11 +423,21 @@
             dma((columns // tile, n_heads)),
             dma((columns // tile, n_heads)),
             dma((kv,)),
+            dma((2,)),
         ],
         compiler_params=pltpu.CompilerParams(
             collective_id=0, has_side_effects=True, vmem_limit_bytes=60 * 1024 * 1024
         ),
-    )(grouped, limits, keys, values, own_keys, own_values, out_weight)
+    )(
+        positions,
+        cached_length,
+        queries.reshape(rows * local_heads, head),
+        cache_keys.reshape(block * kv, head),
+        cache_values.reshape(block * kv, head),
+        new_keys.reshape(rows * kv, head),
+        new_values.reshape(rows * kv, head),
+        out_weight,
+    )
 
 
 def solution(mesh):

time: 106 us -> 97.4 us (0.919)
  local copies, waits for them, and re-layouts: 13 us -> 1.67 us
  Pallas kernels: 90.9 us -> 94.9 us
    unnamed x7 -> x1, local copies, waits for them, and re-layouts: 10.5 us -> 1.67 us
    pallas_call x1, Pallas kernels: 90.9 us -> 94.9 us  [local(): pl.pallas_call(functools.partial(kernel, sizes), out_shape=jax.ShapeDtype...]
    reshape x1 -> x0, local copies, waits for them, and re-layouts: 1.82 us -> none  [local(): queries.reshape(rows, kv, per_group, head).transpose(1, 2, 0, 3)]
where the time goes in v2:
time: 97.4 us; the launch traced here: 97.3 us
  Pallas kernels  94.9 us (97%)
  local copies, waits for them, and re-layouts  1.67 us (2%)
    pallas_call x1, Pallas kernels, local(): pl.pallas_call(functools.partial(kernel, sizes), out_shape=jax.ShapeDtype...  94.9 us

profile of v2, /device:TPU:0, one launch (start us, length us, event | category | flops | bytes accessed | tf_op | source)
XLA Modules:
  0.0 97.3 jit_solution(5591836531591361001)
XLA Ops:
  0.7 94.9 %shard_map.82 = bf16[64,2048]{1,0:T(8,128)(2,1)} custom-call(s32[16]{0:T(128)} %pos_ref.1, s32[1]{0:T(128)S(6)} %copy.10.len_ref, bf16[1024,128]{1,0:T(8,128)(2,1)} %bitcast.7, bf16[8192,128]{1,0:T(8,128)(2,1)} %bitcast.5, bf16[8192,128]{1,0:T(8,128)(2,1)} %bitcast.6, bf16[64,128]{1,0:T(8,128)(2,1)} %bitcast.8, bf16[64,128]{1,0:T(8,128)(2,1)} %bitcast.9, ...), custom_call_target="tpu_custom_call" | custom-call | tf_op jit(solution)/shard_map/pallas_call | solution.py:388
  95.6 1.7 %copy.11 = bf16[64,2048]{1,0:T(8,128)(2,1)} copy(bf16[64,2048]{1,0:T(8,128)(2,1)} %shard_map.82) | data formatting | bytes 524288

commit v3 on v2

--- a/solution.py
+++ b/solution.py
@@ -94,8 +94,8 @@
         for h in range(per_group):
             picked = wide[pl.ds(k * per_group + h, rows, stride=heads_here), :]
             qg[k, z, h * rows : (h + 1) * rows, :] = picked.astype(jnp.bfloat16)
-    lane_token = lax.rem(lax.broadcasted_iota(jnp.int32, (8, lanes), 1), rows)
-    limit_row = jnp.zeros((8, lanes), jnp.int32)
+    lane_token = lax.rem(lax.broadcasted_iota(jnp.int32, (1, lanes), 1), rows)
+    limit_row = jnp.zeros((1, lanes), jnp.int32)
     for t in range(rows):
         limit_row = jnp.where(lane_token == t, jnp.minimum(len_ref[0], pos_ref[t]), limit_row)
     limg[z] = limit_row
@@ -112,7 +112,8 @@
         def _():
             q_copy(k, z, 1).start()
 
-    send_own(0)
+    for k in range(min(2, kv)):
+        send_own(k)
     for step in range(1, n_ctx):
         lim_copy(z, lax.rem(z + step, n_ctx)).start()
 
@@ -141,7 +142,7 @@
 
     def attend(k, s):
         query = qg[k, s]
-        limit = limg[s][0:1, :] - z * block
+        limit = limg[s] - z * block
         peak = jnp.full((1, lanes), FLOOR, jnp.float32)
         for c in range(block // piece):
             span = slice(c * piece, (c + 1) * piece)
@@ -157,64 +158,58 @@
             weights = jnp.exp2((scores[span, :] - peak) * factor)
             total = total + jnp.sum(weights, axis=0, keepdims=True)
             output = output + jnp.dot(val_ref[k, :, span], weights.astype(jnp.bfloat16), preferred_element_type=jnp.float32)
-        row = lax.broadcasted_iota(jnp.int32, (8, lanes), 0)
-        stats = jnp.where(row == 0, peak, total)
 
         @pl.when(s == z)
         def _():
             precv[k, z] = output.astype(jnp.bfloat16)
-            srecv[k, z] = stats
+            srecv[k, z, 0:1, :] = peak
+            srecv[k, z, 1:2, :] = total
 
         @pl.when(s != z)
         def _():
             psend[k, s] = output.astype(jnp.bfloat16)
-            ssend[k, s] = stats
+            ssend[k, s, 0:1, :] = peak
+            ssend[k, s, 1:2, :] = total
             p_copy(k, s).start()
             s_copy(k, s).start()
 
-    def attention(k):
-        @pl.when(k + 1 < kv)
-        def _():
-            send_own(k + 1)
-
-        def visit(i, carry):
-            @pl.when(jnp.logical_and(i > 0, z - i >= 0))
-            def _():
-                q_copy(k, z - i, 0).wait_recv()
-
-                @pl.when(right)
-                def _():
-                    q_copy(k, z - i, 0).start()
-
-                @pl.when(k == 0)
-                def _():
-                    lim_copy(z - i, z - i).wait_recv()
-
-            @pl.when(jnp.logical_and(i > 0, z + i < n_ctx))
-            def _():
-                q_copy(k, z + i, 1).wait_recv()
-
-                @pl.when(left)
-                def _():
-                    q_copy(k, z + i, 1).start()
-
-                @pl.when(k == 0)
-                def _():
-                    lim_copy(z + i, z + i).wait_recv()
-
-            def side(j, inner):
-                s = z - i + 2 * i * j
-                real = jnp.logical_and(s >= 0, s < n_ctx)
-
-                @pl.when(jnp.logical_and(real, jnp.logical_or(i > 0, j == 0)))
-                def _():
-                    attend(k, s)
-
-                return inner
-
-            return lax.fori_loop(0, 2, side, carry)
-
-        lax.fori_loop(0, n_ctx, visit, 0)
+    def q_hop(k, i):
+        @pl.when(z - i >= 0)
+        def _():
+            q_copy(k, z - i, 0).wait_recv()
+
+            @pl.when(right)
+            def _():
+                q_copy(k, z - i, 0).start()
+
+            @pl.when(k == 0)
+            def _():
+                lim_copy(z - i, z - i).wait_recv()
+
+        @pl.when(z + i < n_ctx)
+        def _():
+            q_copy(k, z + i, 1).wait_recv()
+
+            @pl.when(left)
+            def _():
+                q_copy(k, z + i, 1).start()
+
+            @pl.when(k == 0)
+            def _():
+                lim_copy(z + i, z + i).wait_recv()
+
+    def visit(k, i):
+        def side(j, inner):
+            s = z - i + 2 * i * j
+            real = jnp.logical_and(s >= 0, s < n_ctx)
+
+            @pl.when(jnp.logical_and(real, jnp.logical_or(i > 0, j == 0)))
+            def _():
+                attend(k, s)
+
+            return inner
+
+        lax.fori_loop(0, 2, side, 0)
 
     def merge(k):
         for step in range(1, n_ctx):
@@ -260,33 +255,30 @@
         for step in range(1, n_rep):
             c_copy(k, z, step).start()
 
-    def collect(k):
-        def hop(i, carry):
-            @pl.when(z - i >= 0)
-            def _():
-                a_copy(k, z - i, 0).wait_recv()
-
-                @pl.when(right)
-                def _():
-                    a_copy(k, z - i, 0).start()
-
-                for step in range(1, n_rep):
-                    c_copy(k, z - i, step).start()
-
-            @pl.when(z + i < n_ctx)
-            def _():
-                a_copy(k, z + i, 1).wait_recv()
-
-                @pl.when(left)
-                def _():
-                    a_copy(k, z + i, 1).start()
-
-                for step in range(1, n_rep):
-                    c_copy(k, z + i, step).start()
-
-            return carry
-
-        lax.fori_loop(1, n_ctx, hop, 0)
+    def a_hop(k, i):
+        @pl.when(z - i >= 0)
+        def _():
+            a_copy(k, z - i, 0).wait_recv()
+
+            @pl.when(right)
+            def _():
+                a_copy(k, z - i, 0).start()
+
+            for step in range(1, n_rep):
+                c_copy(k, z - i, step).start()
+
+        @pl.when(z + i < n_ctx)
+        def _():
+            a_copy(k, z + i, 1).wait_recv()
+
+            @pl.when(left)
+            def _():
+                a_copy(k, z + i, 1).start()
+
+            for step in range(1, n_rep):
+                c_copy(k, z + i, step).start()
+
+    def gathered(k):
         for step in range(1, n_rep):
             for s in range(n_ctx):
                 c_arrival(k, s, step).wait_recv()
@@ -302,23 +294,42 @@
     acc[...] = jnp.zeros_like(acc)
 
     def stage(k, carry):
-        @pl.when(k < kv)
-        def _():
-            attention(k)
-
-        @pl.when(k >= 1)
-        def _():
-            merge(k - 1)
+        @pl.when(k + 2 < kv)
+        def _():
+            send_own(k + 2)
+
+        def step_of(i, inner):
+            @pl.when(jnp.logical_and(k < kv, i > 0))
+            def _():
+                q_hop(k, i)
+
+            @pl.when(jnp.logical_and(k >= 2, i > 0))
+            def _():
+                a_hop(k - 2, i)
+
+            @pl.when(jnp.logical_and(jnp.logical_and(k >= 1, k <= kv), i == n_ctx // 2))
+            def _():
+                merge(k - 1)
+
+            @pl.when(k < kv)
+            def _():
+                visit(k, i)
+
+            return inner
+
+        lax.fori_loop(0, n_ctx, step_of, 0)
 
         @pl.when(k >= 2)
         def _():
-            collect(k - 2)
+            gathered(k - 2)
+
+        @pl.when(jnp.logical_and(k >= 2, k <= kv))
+        def _():
             lax.fori_loop(0, columns // tile, lambda t, c: (product(k - 2, t), c)[1], 0)
 
         return carry
 
-    lax.fori_loop(0, kv + 1, stage, 0)
-    collect(kv - 1)
+    lax.fori_loop(0, kv + 2, stage, 0)
     for t in range(columns // tile):
         product(kv - 1, t)
         for other in range(n_heads):
@@ -397,12 +408,12 @@
             pltpu.VMEM((kv, block, head), jnp.bfloat16),
             pltpu.VMEM((kv, head, block), jnp.bfloat16),
             pltpu.VMEM((kv, n_ctx, lanes, head), jnp.bfloat16),
-            pltpu.VMEM((n_ctx, 8, lanes), jnp.int32),
+            pltpu.VMEM((n_ctx, 1, lanes), jnp.int32),
             pltpu.VMEM((block, lanes), jnp.float32),
             pltpu.VMEM((kv, n_ctx, head, lanes), jnp.bfloat16),
             pltpu.VMEM((kv, n_ctx, head, lanes), jnp.bfloat16),
-            pltpu.VMEM((kv, n_ctx, 8, lanes), jnp.float32),
-            pltpu.VMEM((kv, n_ctx, 8, lanes), jnp.float32),
+            pltpu.VMEM((kv, n_ctx, 2, lanes), jnp.float32),
+            pltpu.VMEM((kv, n_ctx, 2, lanes), jnp.float32),
             pltpu.VMEM((kv, n_ctx, n_rep, rows, depth), jnp.bfloat16),
             pltpu.VMEM((tokens, columns), jnp.float32),
             pltpu.VMEM((n_heads, out_rows, columns), jnp.bfloat16),

time: 97.4 us -> 86.6 us (0.89)
  Pallas kernels: 94.9 us -> 84.2 us
    pallas_call x1, Pallas kernels: 94.9 us -> 84.2 us  [local(): pl.pallas_call(functools.partial(kernel, sizes), out_shape=jax.ShapeDtype...]
where the time goes in v3:
time: 86.6 us; the launch traced here: 86.5 us
  Pallas kernels  84.2 us (97%)
  local copies, waits for them, and re-layouts  1.67 us (2%)
    pallas_call x1, Pallas kernels, local(): pl.pallas_call(functools.partial(kernel, sizes), out_shape=jax.ShapeDtype...  84.2 us

profile of v3, /device:TPU:0, one launch (start us, length us, event | category | flops | bytes accessed | tf_op | source)
XLA Modules:
  0.0 86.5 jit_solution(4594846340352766534)
XLA Ops:
  0.7 84.2 %shard_map.82 = bf16[64,2048]{1,0:T(8,128)(2,1)} custom-call(s32[16]{0:T(128)} %pos_ref.1, s32[1]{0:T(128)S(6)} %copy.10.len_ref, bf16[1024,128]{1,0:T(8,128)(2,1)} %bitcast.7, bf16[8192,128]{1,0:T(8,128)(2,1)} %bitcast.5, bf16[8192,128]{1,0:T(8,128)(2,1)} %bitcast.6, bf16[64,128]{1,0:T(8,128)(2,1)} %bitcast.8, bf16[64,128]{1,0:T(8,128)(2,1)} %bitcast.9, ...), custom_call_target="tpu_custom_call" | custom-call | tf_op jit(solution)/shard_map/pallas_call | solution.py:399
  84.8 1.7 %copy.11 = bf16[64,2048]{1,0:T(8,128)(2,1)} copy(bf16[64,2048]{1,0:T(8,128)(2,1)} %shard_map.82) | data formatting | bytes 524288

commit v4 on v3

--- a/solution.py
+++ b/solution.py
@@ -16,8 +16,8 @@
 
 def kernel(
     sizes, pos_ref, len_ref, q_ref, ck_ref, cv_ref, nk_ref, nv_ref, w_ref, out_ref,
-    wide, kraw, vraw, key_ref, val_ref, qg, limg, scores, psend, precv, ssend, srecv, att, acc, xsend, xrecv, wbuf,
-    q_ss, q_rs, l_ss, l_rs, p_ss, p_rs, s_ss, s_rs, a_ss, a_rs, c_ss, c_rs, x_ss, x_rs, w_sem, kv_sem,
+    wide, kraw, vraw, key_ref, val_ref, qg, limg, scores, psend, precv, ssend, srecv, pown, ptmp, stmp, att, acc, xsend, xrecv, wbuf,
+    q_ss, q_rs, l_ss, l_rs, p_ss, p_rs, s_ss, s_rs, a_ss, a_rs, c_ss, c_rs, x_ss, x_rs, w_sem, kv_sem, t_rs, u_rs,
 ):
     n_ctx, n_rep, n_heads, kv, rows, per_group, head, block = sizes
     z, r, x = lax.axis_index("ctx"), lax.axis_index("rep"), lax.axis_index("heads")
@@ -54,6 +54,18 @@
 
     def s_arrival(k, s):
         return remote(ssend.at[k, s], srecv.at[k, s], s_ss.at[k, s], s_rs.at[k, s], ctx=s)
+
+    pair = z // 2
+    partner = z + 1 - 2 * lax.rem(z, 2)
+
+    def t_copy(k, s):
+        return remote(psend.at[k, s], ptmp.at[k, s], p_ss.at[k, s], t_rs.at[k, s], ctx=partner)
+
+    def u_copy(k, s):
+        return remote(ssend.at[k, s], stmp.at[k, s], s_ss.at[k, s], u_rs.at[k, s], ctx=partner)
+
+    def nearer(s):
+        return jnp.where(s > z, lax.rem(z, 2) == 1, lax.rem(z, 2) == 0)
 
     def a_copy(k, s, way):
         return remote(att.at[k, s, r], att.at[k, s, r], a_ss.at[k, s, way], a_rs.at[k, s], ctx=z + 1 - 2 * way)
@@ -165,13 +177,51 @@
             srecv[k, z, 0:1, :] = peak
             srecv[k, z, 1:2, :] = total
 
+        inside = s // 2 == pair
+
         @pl.when(s != z)
         def _():
-            psend[k, s] = output.astype(jnp.bfloat16)
             ssend[k, s, 0:1, :] = peak
             ssend[k, s, 1:2, :] = total
+
+        @pl.when(jnp.logical_and(s != z, jnp.logical_or(inside, jnp.logical_not(nearer(s)))))
+        def _():
+            psend[k, s] = output.astype(jnp.bfloat16)
+
+        @pl.when(jnp.logical_and(s != z, inside))
+        def _():
             p_copy(k, s).start()
             s_copy(k, s).start()
+
+        @pl.when(jnp.logical_and(jnp.logical_not(inside), jnp.logical_not(nearer(s))))
+        def _():
+            t_copy(k, s).start()
+            u_copy(k, s).start()
+
+        @pl.when(jnp.logical_and(jnp.logical_not(inside), nearer(s)))
+        def _():
+            pown[lax.rem(k, 2), s] = output
+
+    def forward(k):
+        def each(s, carry):
+            @pl.when(jnp.logical_and(s // 2 != pair, nearer(s)))
+            def _():
+                t_copy(k, s).wait_recv()
+                u_copy(k, s).wait_recv()
+                mine, theirs = ssend[k, s, 0:1, :], stmp[k, s, 0:1, :]
+                top = jnp.maximum(mine, theirs)
+                mine, theirs = jnp.exp2((mine - top) * factor), jnp.exp2((theirs - top) * factor)
+                total = mine * ssend[k, s, 1:2, :] + theirs * stmp[k, s, 1:2, :]
+                output = mine * pown[lax.rem(k, 2), s] + theirs * ptmp[k, s].astype(jnp.float32)
+                psend[k, s] = output.astype(jnp.bfloat16)
+                ssend[k, s, 0:1, :] = top
+                ssend[k, s, 1:2, :] = total
+                p_copy(k, s).start()
+                s_copy(k, s).start()
+
+            return carry
+
+        lax.fori_loop(0, n_ctx, each, 0)
 
     def q_hop(k, i):
         @pl.when(z - i >= 0)
@@ -212,10 +262,13 @@
         lax.fori_loop(0, 2, side, 0)
 
     def merge(k):
-        for step in range(1, n_ctx):
-            s = lax.rem(z + step, n_ctx)
+        sources = []
+        for b in range(n_ctx // 2):
+            s = jnp.where(b < pair, 2 * b + 1, jnp.where(b > pair, 2 * b, partner))
             p_arrival(k, s).wait_recv()
             s_arrival(k, s).wait_recv()
+            sources.append(s)
+        sources.append(z)
         query = qg[k, z]
         wide[: rows * kv, :] = nk_ref[...].astype(jnp.float32)
         own_key = wide[pl.ds(k, rows, stride=kv), :].astype(jnp.bfloat16)
@@ -231,12 +284,12 @@
             preferred_element_type=jnp.float32,
         )
         top = own
-        for b in range(n_ctx):
+        for b in sources:
             top = jnp.maximum(top, srecv[k, b, 0:1, :])
         share = jnp.exp2((own - top) * factor)
         below = share
         above = share * own_value
-        for b in range(n_ctx):
+        for b in sources:
             share = jnp.exp2((srecv[k, b, 0:1, :] - top) * factor)
             below = below + share * srecv[k, b, 1:2, :]
             above = above + share * precv[k, b].astype(jnp.float32)
@@ -307,7 +360,11 @@
             def _():
                 a_hop(k - 2, i)
 
-            @pl.when(jnp.logical_and(jnp.logical_and(k >= 1, k <= kv), i == n_ctx // 2))
+            @pl.when(jnp.logical_and(jnp.logical_and(k >= 1, k <= kv), i == 1))
+            def _():
+                forward(k - 1)
+
+            @pl.when(jnp.logical_and(jnp.logical_and(k >= 1, k <= kv), i == n_ctx - 1))
             def _():
                 merge(k - 1)
 
@@ -414,6 +471,9 @@
             pltpu.VMEM((kv, n_ctx, head, lanes), jnp.bfloat16),
             pltpu.VMEM((kv, n_ctx, 2, lanes), jnp.float32),
             pltpu.VMEM((kv, n_ctx, 2, lanes), jnp.float32),
+            pltpu.VMEM((2, n_ctx, head, lanes), jnp.float32),
+            pltpu.VMEM((kv, n_ctx, head, lanes), jnp.bfloat16),
+            pltpu.VMEM((kv, n_ctx, 2, lanes), jnp.float32),
             pltpu.VMEM((kv, n_ctx, n_rep, rows, depth), jnp.bfloat16),
             pltpu.VMEM((tokens, columns), jnp.float32),
             pltpu.VMEM((n_heads, out_rows, columns), jnp.bfloat16),
@@ -435,6 +495,8 @@
             dma((columns // tile, n_heads)),
             dma((kv,)),
             dma((2,)),
+            dma((kv, n_ctx)),
+            dma((kv, n_ctx)),
         ],
         compiler_params=pltpu.CompilerParams(
             collective_id=0, has_side_effects=True, vmem_limit_bytes=60 * 1024 * 1024

time: 86.6 us -> 96.3 us (1.11)
  Pallas kernels: 84.2 us -> 93.8 us
    pallas_call x1, Pallas kernels: 84.2 us -> 93.8 us  [local(): pl.pallas_call(functools.partial(kernel, sizes), out_shape=jax.ShapeDtype...]
where the time goes in v4:
time: 96.3 us; the launch traced here: 96.1 us
  Pallas kernels  93.8 us (97%)
  local copies, waits for them, and re-layouts  1.67 us (2%)
    pallas_call x1, Pallas kernels, local(): pl.pallas_call(functools.partial(kernel, sizes), out_shape=jax.ShapeDtype...  93.8 us

profile of v4, /device:TPU:0, one launch (start us, length us, event | category | flops | bytes accessed | tf_op | source)
XLA Modules:
  0.0 96.1 jit_solution(3808660745866732027)
XLA Ops:
  0.7 93.8 %shard_map.82 = bf16[64,2048]{1,0:T(8,128)(2,1)} custom-call(s32[16]{0:T(128)} %pos_ref.1, s32[1]{0:T(128)S(6)} %copy.10.len_ref, bf16[1024,128]{1,0:T(8,128)(2,1)} %bitcast.7, bf16[8192,128]{1,0:T(8,128)(2,1)} %bitcast.5, bf16[8192,128]{1,0:T(8,128)(2,1)} %bitcast.6, bf16[64,128]{1,0:T(8,128)(2,1)} %bitcast.8, bf16[64,128]{1,0:T(8,128)(2,1)} %bitcast.9, ...), custom_call_target="tpu_custom_call" | custom-call | tf_op jit(solution)/shard_map/pallas_call | solution.py:456
  94.5 1.7 %copy.11 = bf16[64,2048]{1,0:T(8,128)(2,1)} copy(bf16[64,2048]{1,0:T(8,128)(2,1)} %shard_map.82) | data formatting | bytes 524288
